TPU v7x, 512 devices: a whole 4x8x8 slice. The times are simulated.
512 devices in a mesh: doc: 4 (over x), topic: 16 (over z, core), vocab: 8 (over y).
Axes of the slice: x: 4, y: 8, z: 8, core: 2. Of those that a mesh axis runs over, the one named last changes fastest.
Arguments:
- doc_topics: bfloat16 [2048, 16384], P('doc', 'topic'), may hold values from 0 to 1, as said below
- word_logits: bfloat16 [2048, 16384], P('vocab', 'topic'), may hold values from -6 to 11
- log_norm: float32 [16384], P('topic'), may hold values from 12 to 16
- tile_doc: int32 [512], P(('doc', 'vocab')), may hold values from 0 to 3, as said below
- tile_word: int32 [512], P(('doc', 'vocab')), may hold values from 0 to 3
- word_counts: int32 [512, 64, 128], P(('doc', 'vocab')), may hold values from 0 to 3, as said below
Outputs:
- doc_topic_grad: float32 [2048, 16384], P('doc', ('topic', 'vocab'))
- word_logit_grad: bfloat16 [2048, 16384], P('vocab', 'topic')
Inputs may be any that keep to these rules, and one draw needn't show every extreme that they name: `doc_topics`: each document's row is a softmax over the 16384 topics. Within the 16 slots of one doc and vocab index pair no (tile_doc, tile_word) pair repeats. `word_counts`: A slot whose counts are all zero is empty; occupied slots come first in each pair's list, and in every draw some pair has all 16 slots occupied.
All inputs are finite; a program needn't handle non-finite values.
Results may differ from a plain program's by a relative error of at most 0.018.
Values may be sent and summed in bfloat16 or wider, within the bound.
A program may use at most 64 MiB of HBM per device.

v0:
```python
import jax
import jax.numpy as jnp
from jax import lax
from jax.sharding import PartitionSpec as P

tiles_per_step = 8


def on_device(doc_topics, word_logits, log_norm, tile_doc, tile_word, word_counts):
    tile_total, word_span, doc_span = word_counts.shape
    topic_width = doc_topics.shape[1]
    word_prob = jnp.exp(word_logits.astype(jnp.float32) - log_norm[None, :]).astype(jnp.bfloat16)
    topic_blocks = doc_topics.reshape(-1, doc_span, topic_width)
    prob_blocks = word_prob.reshape(-1, word_span, topic_width)
    doc_rows = topic_blocks[tile_doc]
    word_rows = prob_blocks[tile_word]
    word_part = word_rows
    doc_part = doc_rows
    rate_full = lax.psum(
        jnp.einsum("gwk,gdk->gwd", word_part, doc_part, preferred_element_type=jnp.float32).astype(
            jnp.bfloat16
        ),
        "topic",
    ).astype(jnp.float32)
    ratios = (word_counts.astype(jnp.float32) / (word_span * rate_full)).astype(jnp.bfloat16)

    def accumulate(state_pair, group_index):
        theta_acc, beta_acc = state_pair
        first_row = group_index * tiles_per_step
        ratio_part = lax.dynamic_slice_in_dim(ratios, first_row, tiles_per_step, 0)
        word_part = lax.dynamic_slice_in_dim(word_rows, first_row, tiles_per_step, 0)
        doc_part = lax.dynamic_slice_in_dim(doc_rows, first_row, tiles_per_step, 0)
        doc_index = lax.dynamic_slice_in_dim(tile_doc, first_row, tiles_per_step, 0)
        word_index = lax.dynamic_slice_in_dim(tile_word, first_row, tiles_per_step, 0)
        toward_theta = jnp.einsum(
            "gwd,gwk->gdk", ratio_part, word_part, preferred_element_type=jnp.float32
        )
        toward_beta = jnp.einsum(
            "gwd,gdk->gwk", ratio_part, doc_part, preferred_element_type=jnp.float32
        )
        return (
            (theta_acc.at[doc_index].add(toward_theta), beta_acc.at[word_index].add(toward_beta)),
            None,
        )

    initial = (
        jnp.zeros(topic_blocks.shape, jnp.float32),
        jnp.zeros(prob_blocks.shape, jnp.float32),
    )
    steps_all = jnp.arange(tile_total // tiles_per_step, dtype=jnp.int32)
    (theta_acc, beta_acc), _ = lax.scan(accumulate, initial, steps_all)
    theta_term = -theta_acc.reshape(doc_topics.shape)
    doc_topic_grad = lax.psum_scatter(
        theta_term.astype(jnp.bfloat16), "vocab", scatter_dimension=1, tiled=True
    ).astype(jnp.float32)
    beta_term = -word_prob.astype(jnp.float32) * beta_acc.reshape(word_prob.shape)
    word_logit_grad = lax.psum(beta_term.astype(jnp.bfloat16), "doc")
    return (doc_topic_grad, word_logit_grad)


def solution(mesh):
    placed = (
        P("doc", "topic"),
        P("vocab", "topic"),
        P("topic"),
        P(("doc", "vocab")),
        P(("doc", "vocab")),
        P(("doc", "vocab"), None, None),
    )
    return jax.shard_map(
        on_device,
        mesh=mesh,
        in_specs=placed,
        out_specs=(P("doc", ("topic", "vocab")), P("vocab", "topic")),
        check_vma=False,
    )
```

profile of v0, /device:TPU:1, one launch (start us, length us, event | category | flops | bytes accessed | tf_op | source)
XLA Modules:
  0.0 287.7 jit_solution(454875629672425945)
XLA Ops:
  7.2 0.7 compare_select_fusion.2
  8.0 0.7 compare_select_fusion.3
  8.6 2.0 exponential_convert_fusion
  10.6 1.7 gather_fusion
  12.4 2.8 gather_fusion.1
  15.1 4.4 %convolution_convert_fusion = bf16[16,64,128]{2,1,0:T(8,128)(2,1)} fusion(bf16[16,64,1024]{2,1,0:T(8,128)(2,1)S(1)} %gather_fusion, bf16[16,128,1024]{2,1,0:T(8,128)(2,1)} %gather_fusion.1), kind=kOutput, calls=%fused_computation.15 | convolution fusion | flops 268566528 | bytes 6553600 | tf_op jit(solution)/shard_map/gwk,gdk->gwd/dot_general | solution.py:20
  19.7 120.4 %all-reduce.3.cloned.1.call-done = bf16[16,64,128]{2,1,0:T(8,128)(2,1)} async-done(((bf16[16,64,128]{2,1,0:T(8,128)(2,1)}), bf16[16,64,128]{2,1,0:T(8,128)(2,1)}) %all-reduce.3.cloned.1.call-update) | async-done | bytes 262160 | tf_op jit(solution)/shard_map/psum | solution.py:19
  140.0 1.2 divide_convert_fusion
  141.3 1.1 broadcast_in_dim.20
  142.4 0.2 broadcast_in_dim.19
  142.7 38.2 %while.12 = (s32[]{:T(128)}, f32[4,128,1024]{2,1,0:T(8,128)S(1)}, f32[4,64,1024]{2,1,0:T(8,128)}, s32[2]{0:T(128)S(1)}, s32[16]{0:T(128)S(1)}, /*index=5*/bf16[1...) while((s32[]{:T(128)}, f32[4,128,1024]{2,1,0:T(8,128)S(1)}, ...), condition=%wide.region_4.5_spmd, body=%wide.region_1.4_spmd.sunk | while | flops 270008384 | bytes 28576132 | solution.py:51
  142.7 0.6 dynamic_slice.40
  143.9 0.1 compare_select_fusion.5
  144.0 3.3 %fusion.22 = f32[8,64,1024]{2,1,0:T(8,128)} fusion(bf16[16,128,1024]{2,1,0:T(8,128)(2,1)} %get-tuple-element.165, s32[]{:T(128)S(6)} %select_n.28, bf16[16,64,128]{2,1,0:T(8,128)(2,1)S(1)} %get-tuple-element.162), kind=kOutput, calls=%fused_computation.4.clone.1 | convolution fusion | flops 134217728 | bytes 4326400 | tf_op jit(solution)/shard_map/while/body/eval_jaxpr/gwd,gdk->gwk/dot_general | solution.py:38
  147.3 4.8 %scatter_fusion.1 = f32[4,64,1024]{2,1,0:T(8,128)} fusion(f32[4,64,1024]{2,1,0:T(8,128)} %get-tuple-element.146, s32[8]{0:T(128)S(1)} %get-tuple-element.130, f32[8,64,1024]{2,1,0:T(8,128)} %fusion.22), kind=kCustom, calls=%fused_computation.3.clone.1 | custom fusion | flops 524288 | bytes 6291488 | tf_op jit(solution)/shard_map/while/body/eval_jaxpr/scatter-add | solution.py:42
  152.1 3.9 %fusion.21 = f32[8,128,1024]{2,1,0:T(8,128)} fusion(bf16[16,64,1024]{2,1,0:T(8,128)(2,1)} %get-tuple-element.163, s32[]{:T(128)S(6)} %select_n.28, bf16[16,64,128]{2,1,0:T(8,128)(2,1)S(1)} %get-tuple-element.162), kind=kOutput, calls=%fused_computation.6.clone.1 | convolution fusion | flops 134217728 | bytes 5374976 | tf_op jit(solution)/shard_map/while/body/eval_jaxpr/gwd,gwk->gdk/dot_general | solution.py:35
  156.1 5.7 %scatter_fusion = f32[4,128,1024]{2,1,0:T(8,128)S(1)} fusion(f32[4,128,1024]{2,1,0:T(8,128)S(1)} %get-tuple-element.145, s32[8]{0:T(128)S(1)} %get-tuple-element.129, f32[8,128,1024]{2,1,0:T(8,128)} %fusion.21), kind=kCustom, calls=%fused_computation.2.clone.1 | custom fusion | flops 1048576 | bytes 12582944 | tf_op jit(solution)/shard_map/while/body/eval_jaxpr/scatter-add | solution.py:42
  161.8 0.6 dynamic_slice.40
  163.0 0.1 compare_select_fusion.5
  163.1 3.3 %fusion.22 = f32[8,64,1024]{2,1,0:T(8,128)} fusion(bf16[16,128,1024]{2,1,0:T(8,128)(2,1)} %get-tuple-element.165, s32[]{:T(128)S(6)} %select_n.28, bf16[16,64,128]{2,1,0:T(8,128)(2,1)S(1)} %get-tuple-element.162), kind=kOutput, calls=%fused_computation.4.clone.1 | convolution fusion | flops 134217728 | bytes 4326400 | tf_op jit(solution)/shard_map/while/body/eval_jaxpr/gwd,gdk->gwk/dot_general | solution.py:38
  166.4 4.8 %scatter_fusion.1 = f32[4,64,1024]{2,1,0:T(8,128)} fusion(f32[4,64,1024]{2,1,0:T(8,128)} %get-tuple-element.146, s32[8]{0:T(128)S(1)} %get-tuple-element.130, f32[8,64,1024]{2,1,0:T(8,128)} %fusion.22), kind=kCustom, calls=%fused_computation.3.clone.1 | custom fusion | flops 524288 | bytes 6291488 | tf_op jit(solution)/shard_map/while/body/eval_jaxpr/scatter-add | solution.py:42
  171.2 3.9 %fusion.21 = f32[8,128,1024]{2,1,0:T(8,128)} fusion(bf16[16,64,1024]{2,1,0:T(8,128)(2,1)} %get-tuple-element.163, s32[]{:T(128)S(6)} %select_n.28, bf16[16,64,128]{2,1,0:T(8,128)(2,1)S(1)} %get-tuple-element.162), kind=kOutput, calls=%fused_computation.6.clone.1 | convolution fusion | flops 134217728 | bytes 5374976 | tf_op jit(solution)/shard_map/while/body/eval_jaxpr/gwd,gwk->gdk/dot_general | solution.py:35
  175.2 5.7 %scatter_fusion = f32[4,128,1024]{2,1,0:T(8,128)S(1)} fusion(f32[4,128,1024]{2,1,0:T(8,128)S(1)} %get-tuple-element.145, s32[8]{0:T(128)S(1)} %get-tuple-element.129, f32[8,128,1024]{2,1,0:T(8,128)} %fusion.21), kind=kCustom, calls=%fused_computation.2.clone.1 | custom fusion | flops 1048576 | bytes 12582944 | tf_op jit(solution)/shard_map/while/body/eval_jaxpr/scatter-add | solution.py:42
  180.9 1.3 negate_convert_fusion
  182.2 2.4 copy.8
  184.6 0.0 all-reduce.5.cloned.1.call-start
  184.6 1.0 fusion.8
  185.7 35.4 %reduce-scatter.4.cloned.1.call-done = bf16[128,512]{1,0:T(8,128)(2,1)} async-done(((bf16[1024,512]{1,0:T(8,128)(2,1)}), bf16[128,512]{1,0:T(8,128)(2,1)}) %reduce-scatter.4.cloned.1.call-update) | async-done | bytes 131088
  221.1 1.0 copy.9
  222.2 0.7 convert_element_type.41
  222.9 56.4 %all-reduce.5.cloned.1.call-done = bf16[256,1024]{1,0:T(8,128)(2,1)} async-done(((bf16[256,1024]{1,0:T(8,128)(2,1)}), bf16[256,1024]{1,0:T(8,128)(2,1)}) %all-reduce.5.cloned.1.call-update) | async-done | bytes 524304 | tf_op jit(solution)/shard_map/psum | solution.py:57
  279.3 1.9 copy.23
  (22 shorter events, 0.2 us)
Async XLA Ops:
  7.2 5.2 %copy-start = (bf16[512,1024]{1,0:T(8,128)(2,1)S(1)}, bf16[512,1024]{1,0:T(8,128)(2,1)}, u32[]{:S(2)}) copy-start(bf16[512,1024]{1,0:T(8,128)(2,1)} %param.8) | copy-start | bytes 3145732
  7.2 132.9 %all-reduce.3.cloned.1.call-start = ((), (), s32[]{:S(2)}) async-start(), calls=%async_computation.1 | async-start | bytes 524288 | tf_op jit(solution)/shard_map/psum | solution.py:19
  12.4 2.8 copy-start.2
  19.6 201.5 %reduce-scatter.4.cloned.1.call-start = ((), (), s32[]{:S(2)}) async-start(), calls=%async_computation.3 | async-start | bytes 1179648
  19.7 123.0 %copy-start.5 = (s32[16]{0:T(128)S(1)}, s32[16]{0:T(128)}, u32[]{:S(2)}) copy-start(s32[16]{0:T(128)} %param.12) | copy-start | bytes 196
  19.7 123.0 %copy-start.6 = (s32[16]{0:T(128)S(1)}, s32[16]{0:T(128)}, u32[]{:S(2)}) copy-start(s32[16]{0:T(128)} %param.11) | copy-start | bytes 196
  182.2 2.5 copy-start.1
  182.2 2.5 copy-start.3
  182.2 2.5 copy-start.4
  184.6 94.7 %all-reduce.5.cloned.1.call-start = ((), (), s32[]{:S(2)}) async-start(), calls=%async_computation.2 | async-start | bytes 1048576 | tf_op jit(solution)/shard_map/psum | solution.py:57
Sparse Core Ops, SparseCore 0:
  19.7 120.2 all-reduce.2
  184.7 36.4 reduce-scatter.3
  224.2 55.0 all-reduce.4
where the time goes:
time: 290 us; the launch traced here: 288 us
  waiting for transfers between devices  212 us (73%)
  other arithmetic  28.8 us (10%)
  matrix products  19 us (7%)
  between operations  13.9 us (5%)
  local copies, waits for them, and re-layouts  12.3 us (4%)
    psum x1, waiting for transfers between devices, on_device(): lax.psum(jnp.einsum('gwk,gdk->gwd', word_part, doc_part, preferred_elemen...  120 us
    psum x1, waiting for transfers between devices, on_device(): word_logit_grad = lax.psum(beta_term.astype(jnp.bfloat16), 'doc')  56.4 us
    unnamed x4, waiting for transfers between devices  35.5 us
    scatter-add x2, other arithmetic, accumulate(): theta_acc.at[doc_index].add(toward_theta)  11.4 us
    scatter-add x2, other arithmetic, accumulate(): beta_acc.at[word_index].add(toward_beta)  9.56 us
    dot_general x2, matrix products, accumulate(): jnp.einsum('gwd,gwk->gdk', ratio_part, word_part, preferred_element_type=...  7.89 us
    dot_general x2, matrix products, accumulate(): jnp.einsum('gwd,gdk->gwk', ratio_part, doc_part, preferred_element_type=j...  6.67 us
  transfers between devices with their start and end apart: 3, of which 3 were waited for; matrix products, arithmetic and copies ran while one was open for 1% of the time, Pallas kernels for 0%

commit v1 on v0

v1 whole, which is shorter than its diff:
```python
import functools

import jax
import jax.numpy as jnp
from jax import lax
from jax.experimental import pallas as pl
from jax.experimental.pallas import tpu as pltpu
from jax.sharding import PartitionSpec as P

MESH = pl.DeviceIdType.MESH
F32 = jnp.float32
BF16 = jnp.bfloat16
DT = 4
WT = 4
DS = 128
WS = 64
Z_ORDER = (4, 3, 5, 2, 6, 1, 7)
Z_ARRIVE = (1, 7, 2, 6, 3, 5, 4)


def kernel(
    docs_hbm, logits_hbm, norm_ref, tdoc_ref, tword_ref, counts_hbm,
    theta_hbm, beta_hbm,
    docs, logits, counts, wp,
    rate_b, c_in, z_out, z_in, rt, rt_t, rw,
    th, y_out, y_in, th_fin,
    be, x_out, x_in, be_fin,
    load_sem, c_sem, z_sem, g_sem, f_sem, y_send, y_recv, x_send, x_recv, a_send, a_recv, out_sem,
):
    i, t, l = (lax.axis_index(a) for a in ("doc", "topic", "vocab"))
    z, c = lax.div(t, 2), lax.rem(t, 2)
    other = (i, 2 * z + 1 - c, l)

    def z_peer(d):
        return (i, lax.rem(t + 2 * d, 16), l)

    def y_peer(d):
        return (i, t, lax.rem(l + d + 8, 8))

    def x_peer(d):
        return (lax.rem(i + d + 4, 4), t, l)

    loads = [
        pltpu.make_async_copy(logits_hbm, logits, load_sem.at[0]),
        pltpu.make_async_copy(docs_hbm.at[pl.ds(0, 256)], docs.at[pl.ds(0, 256)], load_sem.at[1]),
        pltpu.make_async_copy(docs_hbm.at[pl.ds(256, 256)], docs.at[pl.ds(256, 256)], load_sem.at[2]),
        pltpu.make_async_copy(counts_hbm, counts, load_sem.at[3]),
    ]
    for cp in loads:
        cp.start()

    barrier = pltpu.get_barrier_semaphore()
    partners = [other] + [z_peer(d) for d in range(1, 8)]
    partners += [y_peer(1), y_peer(-1), x_peer(1), x_peer(-1)]
    for dev in partners:
        pl.semaphore_signal(barrier, inc=1, device_id=dev, device_id_type=MESH)

    loads[0].wait()
    wp[...] = jnp.exp(logits[...].astype(F32) - norm_ref[...]).astype(BF16)
    for h in range(2):
        loads[1 + h].wait()
        rate = lax.dot_general(
            wp[...], docs[pl.ds(256 * h, 256), :], (((1,), (1,)), ((), ())), preferred_element_type=F32
        ).astype(BF16)
        for k in range(2):
            for w in range(WT):
                p = (2 * h + k) * WT + w
                rate_b[p % 2, p // 2] = rate[w * WS:(w + 1) * WS, k * DS:(k + 1) * DS]
    loads[3].wait()

    pl.semaphore_wait(barrier, len(partners))

    swap = pltpu.make_async_remote_copy(
        rate_b.at[1 - c], c_in, c_sem.at[0], c_sem.at[1], device_id=other, device_id_type=MESH
    )
    swap.start()
    slot = jnp.int32(0)
    for s in range(tdoc_ref.shape[0]):
        slot = jnp.where(tdoc_ref[s] * WT + tword_ref[s] == t, s, slot)
    count = counts[slot].astype(F32)
    swap.wait()
    z_out[...] = (rate_b[c].astype(F32) + c_in[...].astype(F32)).astype(BF16)

    scatter = []
    for d in Z_ORDER:
        cp = pltpu.make_async_remote_copy(
            z_out.at[lax.rem(z + d, 8)], z_in.at[d - 1], z_sem.at[0, d - 1], z_sem.at[1, d - 1],
            device_id=z_peer(d), device_id_type=MESH,
        )
        cp.start()
        scatter.append((d, cp))
    total = z_out[z].astype(F32)
    waits = dict(scatter)
    for d in (7, 1, 6, 2, 5, 3, 4):
        waits[d].wait_recv()
        total += z_in[d - 1].astype(F32)
    rt[t] = (-count / (WS * total)).astype(BF16)

    def fwd(src_t):
        return pltpu.make_async_remote_copy(
            rt.at[src_t], rt.at[src_t], f_sem.at[0, lax.div(src_t, 2)], f_sem.at[1, lax.div(src_t, 2)],
            device_id=other, device_id_type=MESH,
        )

    gather = {}
    for d in Z_ORDER:
        cp = pltpu.make_async_remote_copy(
            rt.at[t], rt.at[t], g_sem.at[0, d - 1], g_sem.at[1, d - 1],
            device_id=z_peer(d), device_id_type=MESH,
        )
        cp.start()
        gather[d] = cp
    mine = fwd(t)
    mine.start()
    passed = [mine]
    for d in Z_ARRIVE:
        src_t = lax.rem(t - 2 * d + 16, 16)
        pltpu.make_async_remote_copy(
            rt.at[src_t], rt.at[src_t], g_sem.at[0, d - 1], g_sem.at[1, d - 1],
            device_id=z_peer(d), device_id_type=MESH,
        ).wait_recv()
        cp = fwd(src_t)
        cp.start()
        passed.append(cp)
    for q in range(8):
        src_t = 2 * q + 1 - c
        pltpu.make_async_remote_copy(
            rt.at[src_t], rt.at[src_t], f_sem.at[0, q], f_sem.at[1, q], device_id=other, device_id_type=MESH
        ).wait_recv()

    for s in range(DT):
        tile = rt[pl.ds(s * WT, WT)].reshape(WT * WS, DS)
        rw[:, pl.ds(s * DS, DS)] = tile
        rt_t[pl.ds(s * DS, DS), :] = tile.T

    def theta(q):
        cols = pl.ds(pl.multiple_of(q * 128, 128), 128)
        th[q] = lax.dot_general(
            rt_t[...], wp[:, cols], (((1,), (0,)), ((), ())), preferred_element_type=F32
        )

    def beta(e):
        cols = pl.ds(pl.multiple_of(e * 256, 256), 256)
        be[e] = lax.dot_general(
            rw[...], docs[:, cols], (((1,), (0,)), ((), ())), preferred_element_type=F32
        )

    y_early = ((0, 1), (2, 3))
    y_order = ((2, 3, 0, 1), (0, 1, 2, 3))
    pending = []

    def y_copy(way, step, s):
        return pltpu.make_async_remote_copy(
            y_out.at[way, step, s], y_in.at[way, step, s], y_send.at[way, step, s], y_recv.at[way, step, s],
            device_id=y_peer(1 - 2 * way), device_id_type=MESH,
        )

    def y_go(way, step, s):
        sign = 1 - 2 * way
        q = lax.rem(l + sign * (4 - step) + 8, 8)
        v = th[q, pl.ds(s * DS, DS), :]
        if step > 1 or (step == 1 and s in y_early[way]):
            y_copy(way, step - 1, s).wait_recv()
            v = v + y_in[way, step - 1, s].astype(F32)
        y_out[way, step, s] = v.astype(BF16)
        cp = y_copy(way, step, s)
        cp.start()
        pending.append(cp)

    def x_copy(way, step, u):
        return pltpu.make_async_remote_copy(
            x_out.at[way, step, u], x_in.at[way, step, u], x_send.at[way, step, u], x_recv.at[way, step, u],
            device_id=x_peer(1 - 2 * way), device_id_type=MESH,
        )

    def x_go(way, step, u):
        sign = 1 - 2 * way
        e = lax.rem(i + sign * (2 - step) + 4, 4)
        v = be[e, pl.ds(u * WS, WS), :]
        if step == 1 and u in y_early[way]:
            x_copy(way, 0, u).wait_recv()
            v = v + x_in[way, 0, u].astype(F32)
        x_out[way, step, u] = v.astype(BF16)
        cp = x_copy(way, step, u)
        cp.start()
        pending.append(cp)

    def a_copy(way, e, u):
        hop = lax.rem(i - e + 4, 4)
        return pltpu.make_async_remote_copy(
            be_fin.at[e, u], be_fin.at[e, u], a_send.at[way, e, u], a_recv.at[way, e, u],
            device_id=x_peer(1 - 2 * way), device_id_type=MESH,
        )

    writes = []

    def write_beta(e, u):
        cp = pltpu.make_async_copy(
            be_fin.at[e, u],
            beta_hbm.at[pl.ds(u * WS, WS), pl.ds(pl.multiple_of(e * 256, 256), 256)],
            out_sem.at[0, e, u],
        )
        cp.start()
        writes.append(cp)

    theta(lax.rem(l + 4, 8))
    for way in range(2):
        for s in y_early[way]:
            y_go(way, 0, s)
    beta(lax.rem(i + 2, 4))
    for way in range(2):
        for u in y_early[way]:
            x_go(way, 0, u)
    theta(lax.rem(l + 3, 8))
    theta(lax.rem(l + 5, 8))
    for way in range(2):
        for s in y_early[1 - way]:
            y_go(way, 1, s)
    beta(lax.rem(i + 1, 4))
    beta(lax.rem(i + 3, 4))
    for way in range(2):
        for u in y_early[1 - way]:
            x_go(way, 1, u)
    theta(lax.rem(l + 2, 8))
    theta(lax.rem(l + 6, 8))
    beta(i)
    theta(lax.rem(l + 1, 8))
    theta(lax.rem(l + 7, 8))
    theta(l)
    for k in range(2):
        for way in range(2):
            y_go(way, 1, y_early[way][k])
        for way in range(2):
            x_go(way, 1, y_early[way][k])
    for k in range(4):
        for way in range(2):
            y_go(way, 2, y_order[way][k])

    for u in range(4):
        for way in range(2):
            x_copy(way, 1, u).wait_recv()
        v = be[i, pl.ds(u * WS, WS), :] + x_in[0, 1, u].astype(F32) + x_in[1, 1, u].astype(F32)
        w = wp[pl.ds(u * WS, WS), pl.ds(pl.multiple_of(i * 256, 256), 256)].astype(F32)
        be_fin[i, u] = (v * w).astype(BF16)
        for way in range(2):
            cp = a_copy(way, i, u)
            cp.start()
            pending.append(cp)
        write_beta(i, u)
    for k in range(4):
        for way in range(2):
            y_go(way, 3, y_order[way][k])
    for u in range(4):
        for way in range(2):
            e = lax.rem(i - (1 - 2 * way) + 4, 4)
            a_copy(way, e, u).wait_recv()
            if u in y_early[way]:
                cp = a_copy(way, e, u)
                cp.start()
                pending.append(cp)
            write_beta(e, u)
    for k in range(4):
        s = k
        for way in range(2):
            y_copy(way, 3, s).wait_recv()
        th_fin[pl.ds(s * DS, DS), :] = (
            th[l, pl.ds(s * DS, DS), :] + y_in[0, 3, s].astype(F32) + y_in[1, 3, s].astype(F32)
        )
        cp = pltpu.make_async_copy(
            th_fin.at[pl.ds(s * DS, DS)], theta_hbm.at[pl.ds(s * DS, DS)], out_sem.at[1, 0, s]
        )
        cp.start()
        writes.append(cp)
    e = lax.rem(i + 2, 4)
    for way in range(2):
        for u in y_early[way]:
            a_copy(way, e, u).wait_recv()
            write_beta(e, u)

    for cp in [waits[d] for d in Z_ORDER] + [gather[d] for d in Z_ORDER] + passed + pending:
        cp.wait_send()
    for cp in writes:
        cp.wait()


def on_device(doc_topics, word_logits, log_norm, tile_doc, tile_word, word_counts):
    n_docs, width = doc_topics.shape
    n_words = word_logits.shape[0]
    hbm = pl.BlockSpec(memory_space=pltpu.HBM)
    vmem = pl.BlockSpec(memory_space=pltpu.VMEM)
    smem = pl.BlockSpec(memory_space=pltpu.SMEM)
    V, D = pltpu.VMEM, pltpu.SemaphoreType.DMA
    return pl.pallas_call(
        kernel,
        out_shape=(
            jax.ShapeDtypeStruct((n_docs, 128), F32),
            jax.ShapeDtypeStruct((n_words, width), BF16),
        ),
        in_specs=[hbm, hbm, vmem, smem, smem, hbm],
        out_specs=(hbm, hbm),
        scratch_shapes=[
            V((n_docs, width), BF16),
            V((n_words, width), BF16),
            V(word_counts.shape, jnp.int32),
            V((n_words, width), BF16),
            V((2, 8, WS, DS), BF16),
            V((8, WS, DS), BF16),
            V((8, WS, DS), BF16),
            V((7, WS, DS), BF16),
            V((16, WS, DS), BF16),
            V((n_docs, n_words), BF16),
            V((n_words, n_docs), BF16),
            V((8, n_docs, 128), F32),
            V((2, 4, 4, DS, 128), BF16),
            V((2, 4, 4, DS, 128), BF16),
            V((n_docs, 128), F32),
            V((4, n_words, 256), F32),
            V((2, 2, 4, WS, 256), BF16),
            V((2, 2, 4, WS, 256), BF16),
            V((4, 4, WS, 256), BF16),
            D((4,)),
            D((2,)),
            D((2, 7)),
            D((2, 7)),
            D((2, 8)),
            D((2, 4, 4)),
            D((2, 4, 4)),
            D((2, 2, 4)),
            D((2, 2, 4)),
            D((2, 4, 4)),
            D((2, 4, 4)),
            D((2, 4, 4)),
        ],
        compiler_params=pltpu.CompilerParams(
            collective_id=0, has_side_effects=True, vmem_limit_bytes=40 << 20
        ),
        name="decoder_gradients",
    )(doc_topics, word_logits, log_norm.reshape(1, width), tile_doc, tile_word, word_counts)


def solution(mesh):
    placed = (
        P("doc", "topic"),
        P("vocab", "topic"),
        P("topic"),
        P(("doc", "vocab")),
        P(("doc", "vocab")),
        P(("doc", "vocab"), None, None),
    )
    return jax.shard_map(
        on_device,
        mesh=mesh,
        in_specs=placed,
        out_specs=(P("doc", ("topic", "vocab")), P("vocab", "topic")),
        check_vma=False,
    )
```

time: 290 us -> 52.3 us (0.18)
  waiting for transfers between devices: 212 us -> 0 us
  Pallas kernels: 0 us -> 45.2 us
  other arithmetic: 28.8 us -> 0 us
  matrix products: 19 us -> 0 us
  between operations: 13.9 us -> 0.66 us
  local copies, waits for them, and re-layouts: 12.3 us -> 6.15 us
    psum x2 -> x0, waiting for transfers between devices: 177 us -> none  [the longest x1 120 us: on_device(): lax.psum(jnp.einsum('gwk,gdk->gwd', word_part, doc_part, preferred_elemen...]
    pallas_call x0 -> x1, Pallas kernels: none -> 45.2 us  [on_device(): pl.pallas_call(kernel, out_shape=(jax.ShapeDtypeStruct((n_docs, 128), F32...]
    unnamed x4 -> x0, waiting for transfers between devices: 35.5 us -> none
    scatter-add x4 -> x0, other arithmetic: 21 us -> none  [the longest x2 11.4 us: accumulate(): theta_acc.at[doc_index].add(toward_theta)]
    dot_general x5 -> x0, matrix products: 19 us -> none  [the longest x2 7.89 us: accumulate(): jnp.einsum('gwd,gwk->gdk', ratio_part, word_part, preferred_element_type=...]
    convert_element_type x5 -> x0, other arithmetic: 6.25 us -> none  [the longest x1 2 us: on_device(): jnp.exp(word_logits.astype(jnp.float32) - log_norm[None, :])]
    gather x2 -> x0, local copies, waits for them, and re-layouts: 4.48 us -> none  [the longest x1 2.76 us: on_device(): doc_rows = topic_blocks[tile_doc]]
    unnamed x17 -> x14, local copies, waits for them, and re-layouts: 5.31 us -> 6.15 us
  transfers between devices with their start and end apart: 3 -> 0, of which waited for: 3 -> 0; matrix products, arithmetic and copies ran while one was open for 1% -> 0% of each run, Pallas kernels for 0% -> 0%
where the time goes in v1:
time: 52.3 us; the launch traced here: 52 us
  Pallas kernels  45.2 us (86%)
  local copies, waits for them, and re-layouts  6.15 us (12%)
  between operations  0.66 us (1%)
    pallas_call x1, Pallas kernels, on_device(): pl.pallas_call(kernel, out_shape=(jax.ShapeDtypeStruct((n_docs, 128), F32...  45.2 us
    unnamed x14, local copies, waits for them, and re-layouts  6.15 us

profile of v1, /device:TPU:1, one launch (start us, length us, event | category | flops | bytes accessed | tf_op | source)
XLA Modules:
  0.0 52.0 jit_solution(18363728632779987850)
XLA Ops:
  0.6 0.0 copy-start.5
  0.6 0.0 copy-start.4
  0.7 0.6 %copy-done.5 = s32[16]{0:T(128)S(1)} copy-done((s32[16]{0:T(128)S(1)}, s32[16]{0:T(128)}, u32[]{:S(2)}) %copy-start.5) | copy-done | bytes 88
  1.3 0.0 copy-done.4
  1.3 0.0 copy-start
  1.3 1.2 %copy-done = bf16[512,1024]{1,0:T(8,128)(2,1)S(1)} copy-done((bf16[512,1024]{1,0:T(8,128)(2,1)S(1)}, bf16[512,1024]{1,0:T(8,128)(2,1)}, u32[]{:S(2)}) %copy-start) | copy-done | bytes 1048600
  2.5 0.0 copy-start.1
  2.5 1.0 %copy-done.1 = bf16[256,1024]{1,0:T(8,128)(2,1)S(1)} copy-done((bf16[256,1024]{1,0:T(8,128)(2,1)S(1)}, bf16[256,1024]{1,0:T(8,128)(2,1)}, u32[]{:S(2)}) %copy-start.1) | copy-done | bytes 524312
  3.6 0.0 copy-start.2
  3.6 1.0 %copy-done.2 = s32[16,64,128]{2,1,0:T(8,128)S(1)} copy-done((s32[16,64,128]{2,1,0:T(8,128)S(1)}, s32[16,64,128]{2,1,0:T(8,128)}, u32[]{:S(2)}) %copy-start.2) | copy-done | bytes 524312
  4.6 0.0 copy-start.3
  4.6 0.7 %copy-done.3 = f32[1024]{0:T(1024)S(1)} copy-done((f32[1024]{0:T(1024)S(1)}, f32[1024]{0:T(1024)}, u32[]{:S(2)}) %copy-start.3) | copy-done | bytes 4120
  5.3 45.2 %decoder_gradients.1 = (f32[512,128]{1,0:T(8,128)S(1)}, bf16[256,1024]{1,0:T(8,128)(2,1)S(1)}) custom-call(bf16[512,1024]{1,0:T(8,128)(2,1)S(1)} %copy-done, bf16[256,1024]{1,0:T(8,128)(2,1)S(1)} %copy-done.1, f32[1,1024]{1,0:T(1,128)S(1)} %bitcast.1, s32[16]{0:T(128)S(1)} %copy-done.4, s32[16]{0:T(128)S(1)} %copy-done.5, s32[16,64,128]{2,1,0:T(8,128)S(1)} %copy-done.2), custom_call_target="tpu_custom_call" | custom-call | tf_op jit(solution)/shard_map/decoder_gradients/pallas_call | solution.py:293
  50.5 0.7 %copy.10 = f32[512,128]{1,0:T(8,128)} copy(f32[512,128]{1,0:T(8,128)S(1)} %get-tuple-element.4) | data formatting | bytes 524288
  51.2 0.8 %copy.11 = bf16[256,1024]{1,0:T(8,128)(2,1)} copy(bf16[256,1024]{1,0:T(8,128)(2,1)S(1)} %get-tuple-element.5) | data formatting | bytes 1048576
Async XLA Ops:
  0.6 0.7 %copy-start.5 = (s32[16]{0:T(128)S(1)}, s32[16]{0:T(128)}, u32[]{:S(2)}) copy-start(s32[16]{0:T(128)} %tword_ref.1) | copy-start | bytes 196
  0.6 0.7 %copy-start.4 = (s32[16]{0:T(128)S(1)}, s32[16]{0:T(128)}, u32[]{:S(2)}) copy-start(s32[16]{0:T(128)} %tdoc_ref.1) | copy-start | bytes 196
  1.3 1.2 %copy-start = (bf16[512,1024]{1,0:T(8,128)(2,1)S(1)}, bf16[512,1024]{1,0:T(8,128)(2,1)}, u32[]{:S(2)}) copy-start(bf16[512,1024]{1,0:T(8,128)(2,1)} %docs_hbm.1) | copy-start | bytes 3145732
  2.5 1.0 %copy-start.1 = (bf16[256,1024]{1,0:T(8,128)(2,1)S(1)}, bf16[256,1024]{1,0:T(8,128)(2,1)}, u32[]{:S(2)}) copy-start(bf16[256,1024]{1,0:T(8,128)(2,1)} %logits_hbm.1) | copy-start | bytes 1572868
  3.6 1.0 %copy-start.2 = (s32[16,64,128]{2,1,0:T(8,128)S(1)}, s32[16,64,128]{2,1,0:T(8,128)}, u32[]{:S(2)}) copy-start(s32[16,64,128]{2,1,0:T(8,128)} %counts_hbm.1) | copy-start | bytes 1572868
  4.6 0.7 %copy-start.3 = (f32[1024]{0:T(1024)S(1)}, f32[1024]{0:T(1024)}, u32[]{:S(2)}) copy-start(f32[1024]{0:T(1024)} %param.8) | copy-start | bytes 12292

commit v2 on v1

--- a/solution.py
+++ b/solution.py
@@ -19,13 +19,13 @@
 
 
 def kernel(
-    docs_hbm, logits_hbm, norm_ref, tdoc_ref, tword_ref, counts_hbm,
-    theta_hbm, beta_hbm,
-    docs, logits, counts, wp,
+    docs_hbm, logits_hbm, norm_hbm, tdoc_hbm, tword_hbm, counts_hbm,
+    th_fin, be_fin,
+    docs, logits, norm_ref, tdoc_ref, tword_ref, counts, wp,
     rate_b, c_in, z_out, z_in, rt, rt_t, rw,
-    th, y_out, y_in, th_fin,
-    be, x_out, x_in, be_fin,
-    load_sem, c_sem, z_sem, g_sem, f_sem, y_send, y_recv, x_send, x_recv, a_send, a_recv, out_sem,
+    th, y_out, y_in,
+    be, x_out, x_in,
+    load_sem, c_sem, z_sem, g_sem, f_sem, y_send, y_recv, x_send, x_recv, a_send, a_recv,
 ):
     i, t, l = (lax.axis_index(a) for a in ("doc", "topic", "vocab"))
     z, c = lax.div(t, 2), lax.rem(t, 2)
@@ -41,10 +41,13 @@
         return (lax.rem(i + d + 4, 4), t, l)
 
     loads = [
+        pltpu.make_async_copy(norm_hbm, norm_ref, load_sem.at[4]),
         pltpu.make_async_copy(logits_hbm, logits, load_sem.at[0]),
         pltpu.make_async_copy(docs_hbm.at[pl.ds(0, 256)], docs.at[pl.ds(0, 256)], load_sem.at[1]),
         pltpu.make_async_copy(docs_hbm.at[pl.ds(256, 256)], docs.at[pl.ds(256, 256)], load_sem.at[2]),
         pltpu.make_async_copy(counts_hbm, counts, load_sem.at[3]),
+        pltpu.make_async_copy(tdoc_hbm, tdoc_ref, load_sem.at[5]),
+        pltpu.make_async_copy(tword_hbm, tword_ref, load_sem.at[6]),
     ]
     for cp in loads:
         cp.start()
@@ -56,9 +59,10 @@
         pl.semaphore_signal(barrier, inc=1, device_id=dev, device_id_type=MESH)
 
     loads[0].wait()
+    loads[1].wait()
     wp[...] = jnp.exp(logits[...].astype(F32) - norm_ref[...]).astype(BF16)
     for h in range(2):
-        loads[1 + h].wait()
+        loads[2 + h].wait()
         rate = lax.dot_general(
             wp[...], docs[pl.ds(256 * h, 256), :], (((1,), (1,)), ((), ())), preferred_element_type=F32
         ).astype(BF16)
@@ -66,7 +70,8 @@
             for w in range(WT):
                 p = (2 * h + k) * WT + w
                 rate_b[p % 2, p // 2] = rate[w * WS:(w + 1) * WS, k * DS:(k + 1) * DS]
-    loads[3].wait()
+    for cp in loads[4:]:
+        cp.wait()
 
     pl.semaphore_wait(barrier, len(partners))
 
@@ -188,20 +193,9 @@
     def a_copy(way, e, u):
         hop = lax.rem(i - e + 4, 4)
         return pltpu.make_async_remote_copy(
-            be_fin.at[e, u], be_fin.at[e, u], a_send.at[way, e, u], a_recv.at[way, e, u],
+            be_fin.at[e, pl.ds(u * WS, WS)], be_fin.at[e, pl.ds(u * WS, WS)], a_send.at[way, e, u], a_recv.at[way, e, u],
             device_id=x_peer(1 - 2 * way), device_id_type=MESH,
         )
-
-    writes = []
-
-    def write_beta(e, u):
-        cp = pltpu.make_async_copy(
-            be_fin.at[e, u],
-            beta_hbm.at[pl.ds(u * WS, WS), pl.ds(pl.multiple_of(e * 256, 256), 256)],
-            out_sem.at[0, e, u],
-        )
-        cp.start()
-        writes.append(cp)
 
     theta(lax.rem(l + 4, 8))
     for way in range(2):
@@ -241,12 +235,11 @@
             x_copy(way, 1, u).wait_recv()
         v = be[i, pl.ds(u * WS, WS), :] + x_in[0, 1, u].astype(F32) + x_in[1, 1, u].astype(F32)
         w = wp[pl.ds(u * WS, WS), pl.ds(pl.multiple_of(i * 256, 256), 256)].astype(F32)
-        be_fin[i, u] = (v * w).astype(BF16)
+        be_fin[i, pl.ds(u * WS, WS), :] = (v * w).astype(BF16)
         for way in range(2):
             cp = a_copy(way, i, u)
             cp.start()
             pending.append(cp)
-        write_beta(i, u)
     for k in range(4):
         for way in range(2):
             y_go(way, 3, y_order[way][k])
@@ -258,7 +251,6 @@
                 cp = a_copy(way, e, u)
                 cp.start()
                 pending.append(cp)
-            write_beta(e, u)
     for k in range(4):
         s = k
         for way in range(2):
@@ -266,41 +258,47 @@
         th_fin[pl.ds(s * DS, DS), :] = (
             th[l, pl.ds(s * DS, DS), :] + y_in[0, 3, s].astype(F32) + y_in[1, 3, s].astype(F32)
         )
-        cp = pltpu.make_async_copy(
-            th_fin.at[pl.ds(s * DS, DS)], theta_hbm.at[pl.ds(s * DS, DS)], out_sem.at[1, 0, s]
-        )
-        cp.start()
-        writes.append(cp)
     e = lax.rem(i + 2, 4)
     for way in range(2):
         for u in y_early[way]:
             a_copy(way, e, u).wait_recv()
-            write_beta(e, u)
 
     for cp in [waits[d] for d in Z_ORDER] + [gather[d] for d in Z_ORDER] + passed + pending:
         cp.wait_send()
-    for cp in writes:
+
+
+def finish(th_ref, be_ref, theta_hbm, beta_hbm, sem):
+    copies = [pltpu.make_async_copy(th_ref, theta_hbm, sem.at[4])]
+    for e in range(4):
+        copies.append(pltpu.make_async_copy(be_ref.at[e], beta_hbm.at[:, pl.ds(e * 256, 256)], sem.at[e]))
+    for cp in copies:
+        cp.start()
+    for cp in copies:
         cp.wait()
 
 
 def on_device(doc_topics, word_logits, log_norm, tile_doc, tile_word, word_counts):
     n_docs, width = doc_topics.shape
     n_words = word_logits.shape[0]
+    slots = tile_doc.shape[0]
     hbm = pl.BlockSpec(memory_space=pltpu.HBM)
     vmem = pl.BlockSpec(memory_space=pltpu.VMEM)
-    smem = pl.BlockSpec(memory_space=pltpu.SMEM)
     V, D = pltpu.VMEM, pltpu.SemaphoreType.DMA
-    return pl.pallas_call(
+    operands = (doc_topics, word_logits, log_norm.reshape(1, width), tile_doc, tile_word, word_counts)
+    theta, beta = pl.pallas_call(
         kernel,
         out_shape=(
             jax.ShapeDtypeStruct((n_docs, 128), F32),
-            jax.ShapeDtypeStruct((n_words, width), BF16),
+            jax.ShapeDtypeStruct((4, n_words, 256), BF16),
         ),
-        in_specs=[hbm, hbm, vmem, smem, smem, hbm],
-        out_specs=(hbm, hbm),
+        in_specs=[hbm] * 6,
+        out_specs=(vmem, vmem),
         scratch_shapes=[
             V((n_docs, width), BF16),
             V((n_words, width), BF16),
+            V((1, width), F32),
+            pltpu.SMEM((slots,), jnp.int32),
+            pltpu.SMEM((slots,), jnp.int32),
             V(word_counts.shape, jnp.int32),
             V((n_words, width), BF16),
             V((2, 8, WS, DS), BF16),
@@ -313,12 +311,10 @@
             V((8, n_docs, 128), F32),
             V((2, 4, 4, DS, 128), BF16),
             V((2, 4, 4, DS, 128), BF16),
-            V((n_docs, 128), F32),
             V((4, n_words, 256), F32),
             V((2, 2, 4, WS, 256), BF16),
             V((2, 2, 4, WS, 256), BF16),
-            V((4, 4, WS, 256), BF16),
-            D((4,)),
+            D((7,)),
             D((2,)),
             D((2, 7)),
             D((2, 7)),
@@ -329,13 +325,23 @@
             D((2, 2, 4)),
             D((2, 4, 4)),
             D((2, 4, 4)),
-            D((2, 4, 4)),
         ],
         compiler_params=pltpu.CompilerParams(
             collective_id=0, has_side_effects=True, vmem_limit_bytes=40 << 20
         ),
         name="decoder_gradients",
-    )(doc_topics, word_logits, log_norm.reshape(1, width), tile_doc, tile_word, word_counts)
+    )(*(pltpu.with_memory_space_constraint(x, pltpu.HBM) for x in operands))
+    return pl.pallas_call(
+        finish,
+        out_shape=(
+            jax.ShapeDtypeStruct((n_docs, 128), F32),
+            jax.ShapeDtypeStruct((n_words, width), BF16),
+        ),
+        in_specs=[pl.BlockSpec(memory_space=pl.ANY)] * 2,
+        out_specs=(hbm, hbm),
+        scratch_shapes=[D((5,))],
+        name="write_out",
+    )(*(pltpu.with_memory_space_constraint(x, pltpu.VMEM) for x in (theta, beta)))
 
 
 def solution(mesh):

time: 52.3 us -> 46.1 us (0.88)
  local copies, waits for them, and re-layouts: 6.15 us -> 0 us
    unnamed x14 -> x0, local copies, waits for them, and re-layouts: 6.15 us -> none
    pallas_call x0 -> x1, Pallas kernels: none -> 0.92 us  [on_device(): pl.pallas_call(finish, out_shape=(jax.ShapeDtypeStruct((n_docs, 128), F32...]
    pallas_call x1, Pallas kernels: 45.2 us -> 44.4 us  [on_device(): pl.pallas_call(kernel, out_shape=(jax.ShapeDtypeStruct((n_docs, 128), F32...]
where the time goes in v2:
time: 46.1 us; the launch traced here: 45.9 us
  Pallas kernels  45.3 us (98%)
  between operations  0.64 us (1%)
    pallas_call x1, Pallas kernels, on_device(): pl.pallas_call(kernel, out_shape=(jax.ShapeDtypeStruct((n_docs, 128), F32...  44.4 us

profile of v2, /device:TPU:1, one launch (start us, length us, event | category | flops | bytes accessed | tf_op | source)
XLA Modules:
  0.0 45.9 jit_solution(4682726782094377551)
XLA Ops:
  0.6 44.4 %decoder_gradients.1 = (f32[512,128]{1,0:T(8,128)S(1)}, bf16[4,256,256]{2,1,0:T(8,128)(2,1)S(1)}) custom-call(bf16[512,1024]{1,0:T(8,128)(2,1)} %docs_hbm.1, bf16[256,1024]{1,0:T(8,128)(2,1)} %logits_hbm.1, f32[1,1024]{1,0:T(1,128)} %bitcast.1, s32[16]{0:T(128)} %tdoc_hbm.1, s32[16]{0:T(128)} %tword_hbm.1, s32[16,64,128]{2,1,0:T(8,128)} %counts_hbm.1), custom_call_target="tpu_custom_call" | custom-call | tf_op jit(solution)/shard_map/decoder_gradients/pallas_call | solution.py:288
  45.0 0.9 %write_out.1 = (f32[512,128]{1,0:T(8,128)}, bf16[256,1024]{1,0:T(8,128)(2,1)}) custom-call(f32[512,128]{1,0:T(8,128)S(1)} %get-tuple-element.4.th_ref, bf16[4,256,256]{2,1,0:T(8,128)(2,1)S(1)} %get-tuple-element.5.be_ref), custom_call_target="tpu_custom_call" | custom-call | tf_op jit(solution)/shard_map/write_out/pallas_call | solution.py:334

commit v3 on v0

v3 whole, which is shorter than its diff:
```python
import jax
import jax.numpy as jnp
from jax import lax
from jax.experimental import pallas as pl
from jax.experimental.pallas import tpu as pltpu
from jax.sharding import PartitionSpec as P

MESH = pl.DeviceIdType.MESH
F32 = jnp.float32
BF16 = jnp.bfloat16
DT = 4
WT = 4
DS = 128
WS = 64
Z_ORDER = (4, 3, 5, 2, 6, 1, 7)
Z_ARRIVE = (1, 7, 2, 6, 3, 5, 4)


def kernel(
    docs_hbm, logits_hbm, norm_hbm, tdoc_hbm, tword_hbm, counts_hbm,
    th_fin, be_fin,
    docs, logits, norm_ref, tdoc_ref, tword_ref, counts, wp,
    rate_b, c_in, z_out, z_in, rt, rt_t, rw,
    th, y_out, y_in,
    be, x_out, x_in,
    load_sem, c_sem, send_sem, z_recv, g_recv, f_recv, y_recv, x_recv, a_recv,
):
    i, t, l = (lax.axis_index(a) for a in ("doc", "topic", "vocab"))
    z, c = lax.div(t, 2), lax.rem(t, 2)
    loads = [
        pltpu.make_async_copy(norm_hbm, norm_ref, load_sem.at[0]),
        pltpu.make_async_copy(logits_hbm, logits, load_sem.at[1]),
        pltpu.make_async_copy(docs_hbm.at[pl.ds(0, 256)], docs.at[pl.ds(0, 256)], load_sem.at[2]),
        pltpu.make_async_copy(docs_hbm.at[pl.ds(256, 256)], docs.at[pl.ds(256, 256)], load_sem.at[3]),
        pltpu.make_async_copy(counts_hbm, counts, load_sem.at[4]),
        pltpu.make_async_copy(tdoc_hbm, tdoc_ref, load_sem.at[5]),
        pltpu.make_async_copy(tword_hbm, tword_ref, load_sem.at[6]),
    ]
    for cp in loads:
        cp.start()

    other = (i, 2 * z + 1 - c, l)
    z_at = [lax.rem(z + d, 8) for d in range(8)]
    z_to = [(i, 2 * z_at[d] + c, l) for d in range(8)]
    y_at = [lax.rem(l + d, 8) for d in range(8)]
    x_at = [lax.rem(i + d, 4) for d in range(4)]
    y_to = [(i, t, y_at[1]), (i, t, y_at[7])]
    x_to = [(x_at[1], t, l), (x_at[3], t, l)]

    barrier = pltpu.get_barrier_semaphore()
    partners = z_to[1:] + [other] + y_to + x_to
    for dev in partners:
        pl.semaphore_signal(barrier, inc=1, device_id=dev, device_id_type=MESH)

    def remote(src, dst, send, recv, dev):
        return pltpu.make_async_remote_copy(src, dst, send, recv, device_id=dev, device_id_type=MESH)

    loads[0].wait()
    loads[1].wait()
    wp[...] = jnp.exp(logits[...].astype(F32) - norm_ref[...]).astype(BF16)
    for h in range(2):
        loads[2 + h].wait()
        rate = lax.dot_general(
            wp[...], docs[pl.ds(256 * h, 256), :], (((1,), (1,)), ((), ())), preferred_element_type=F32
        ).astype(BF16)
        for k in range(2):
            for w in range(WT):
                p = (2 * h + k) * WT + w
                rate_b[p % 2, p // 2] = rate[w * WS:(w + 1) * WS, k * DS:(k + 1) * DS]
    for cp in loads[4:]:
        cp.wait()

    pl.semaphore_wait(barrier, len(partners))

    swap = remote(rate_b.at[1 - c], c_in, c_sem.at[0], c_sem.at[1], other)
    swap.start()
    slot = jnp.int32(0)
    for s in range(tdoc_ref.shape[0]):
        slot = jnp.where(tdoc_ref[s] * WT + tword_ref[s] == t, s, slot)
    count = counts[slot].astype(F32)
    swap.wait_recv()
    z_out[...] = (rate_b[c].astype(F32) + c_in[...].astype(F32)).astype(BF16)

    for d in Z_ORDER:
        remote(z_out.at[z_at[d]], z_in.at[d - 1], send_sem.at[0], z_recv.at[0], z_to[d]).start()
    total = z_out[z].astype(F32)
    remote(z_in, z_in, send_sem.at[0], z_recv.at[0], other).wait_recv()
    for d in range(1, 8):
        total += z_in[d - 1].astype(F32)
    rt[c, z] = (-count / (WS * total)).astype(BF16)

    mine = rt.at[c, z]
    for d in Z_ORDER:
        remote(mine, mine, send_sem.at[1], g_recv.at[d - 1], z_to[d]).start()
    remote(mine, mine, send_sem.at[2], f_recv.at[0], other).start()
    for d in Z_ARRIVE:
        tile = rt.at[c, z_at[8 - d]]
        remote(tile, tile, send_sem.at[1], g_recv.at[d - 1], other).wait_recv()
        remote(tile, tile, send_sem.at[2], f_recv.at[0], other).start()
    remote(rt.at[1 - c], rt.at[1 - c], send_sem.at[2], f_recv.at[0], other).wait_recv()

    for s in range(DT):
        tiles = [rt[w % 2, 2 * s + w // 2] for w in range(WT)]
        tile = jnp.concatenate(tiles, axis=0)
        rw[:, pl.ds(s * DS, DS)] = tile
        rt_t[pl.ds(s * DS, DS), :] = tile.T

    def theta(d):
        cols = pl.ds(pl.multiple_of(y_at[d] * 128, 128), 128)
        th[y_at[d]] = lax.dot_general(
            rt_t[...], wp[:, cols], (((1,), (0,)), ((), ())), preferred_element_type=F32
        )

    def beta(d):
        cols = pl.ds(pl.multiple_of(x_at[d] * 256, 256), 256)
        be[x_at[d]] = lax.dot_general(
            rw[...], docs[:, cols], (((1,), (0,)), ((), ())), preferred_element_type=F32
        )

    HD, HW = 2 * DS, 2 * WS

    def y_copy(way, step, early):
        k = 7 * way + 2 * step - (0 if early else 1)
        return remote(y_out.at[k], y_in.at[k], send_sem.at[3], y_recv.at[k], y_to[way]), k

    def y_go(step, early):
        for way in range(2):
            h = way if early else 1 - way
            d = 4 - step if way == 0 else 4 + step
            v = th[y_at[d], pl.ds(h * HD, HD), :]
            if step > 1 or (step == 1 and early):
                cp, k = y_copy(way, step - 1, early)
                cp.wait_recv()
                v = v + y_in[k].astype(F32)
            cp, k = y_copy(way, step, early)
            y_out[k] = v.astype(BF16)
            cp.start()

    def x_copy(way, step, early):
        k = 3 * way + 2 * step - (0 if early else 1)
        return remote(x_out.at[k], x_in.at[k], send_sem.at[4], x_recv.at[k], x_to[way]), k

    def x_go(step, early):
        for way in range(2):
            h = way if early else 1 - way
            d = 2 - step if way == 0 else 2 + step
            v = be[x_at[d], pl.ds(h * HW, HW), :]
            if step == 1 and early:
                cp, k = x_copy(way, 0, True)
                cp.wait_recv()
                v = v + x_in[k].astype(F32)
            cp, k = x_copy(way, step, early)
            x_out[k] = v.astype(BF16)
            cp.start()

    def a_copy(way, kind, e):
        h = 1 - way if kind == 1 else way
        rows = be_fin.at[e, pl.ds(h * HW, HW)]
        return remote(rows, rows, send_sem.at[5], a_recv.at[3 * way + kind], x_to[way])

    def beta_whole():
        for h in range(2):
            cp, early = x_copy(h, 1, True)
            cp.wait_recv()
            cp, late = x_copy(1 - h, 1, False)
            cp.wait_recv()
            rows = pl.ds(h * HW, HW)
            v = be[i, rows, :] + x_in[early].astype(F32) + x_in[late].astype(F32)
            w = wp[rows, pl.ds(pl.multiple_of(i * 256, 256), 256)].astype(F32)
            be_fin[i, rows, :] = (v * w).astype(BF16)
            a_copy(h, 0, i).start()
        for way in range(2):
            a_copy(way, 1, i).start()

    def from_way(way):
        return x_at[3] if way == 0 else x_at[1]

    theta(4)
    y_go(0, True)
    beta(2)
    x_go(0, True)
    theta(3)
    theta(5)
    y_go(1, False)
    beta(1)
    beta(3)
    x_go(1, False)
    theta(2)
    theta(6)
    beta(0)
    y_go(1, True)
    x_go(1, True)
    theta(1)
    theta(7)
    theta(0)
    y_go(2, False)
    y_go(2, True)
    beta_whole()
    y_go(3, False)
    y_go(3, True)
    for way in range(2):
        a_copy(way, 0, from_way(way)).wait_recv()
        a_copy(way, 2, from_way(way)).start()
    for h in range(2):
        cp, late = y_copy(1 - h, 3, False)
        cp.wait_recv()
        cp, early = y_copy(h, 3, True)
        cp.wait_recv()
        rows = pl.ds(h * HD, HD)
        th_fin[rows, :] = th[l, rows, :] + y_in[early].astype(F32) + y_in[late].astype(F32)
    for way in range(2):
        a_copy(way, 1, from_way(way)).wait_recv()
    for way in range(2):
        a_copy(way, 2, x_at[2]).wait_recv()

    remote(rate_b.at[1 - c], c_in, c_sem.at[0], c_sem.at[1], other).wait_send()
    remote(z_in, z_in, send_sem.at[0], z_recv.at[0], other).wait_send()
    remote(z_in, z_in, send_sem.at[1], z_recv.at[0], other).wait_send()
    remote(z_out, z_out, send_sem.at[2], z_recv.at[0], other).wait_send()
    remote(y_out, y_in, send_sem.at[3], z_recv.at[0], other).wait_send()
    remote(x_out, x_in, send_sem.at[4], z_recv.at[0], other).wait_send()
    remote(x_out, x_in, send_sem.at[5], z_recv.at[0], other).wait_send()


def finish(th_ref, be_ref, theta_hbm, beta_hbm, sem):
    copies = [pltpu.make_async_copy(th_ref, theta_hbm, sem.at[4])]
    for e in range(4):
        copies.append(pltpu.make_async_copy(be_ref.at[e], beta_hbm.at[:, pl.ds(e * 256, 256)], sem.at[e]))
    for cp in copies:
        cp.start()
    for cp in copies:
        cp.wait()


def on_device(doc_topics, word_logits, log_norm, tile_doc, tile_word, word_counts):
    n_docs, width = doc_topics.shape
    n_words = word_logits.shape[0]
    slots = tile_doc.shape[0]
    hbm = pl.BlockSpec(memory_space=pltpu.HBM)
    vmem = pl.BlockSpec(memory_space=pltpu.VMEM)
    V, D = pltpu.VMEM, pltpu.SemaphoreType.DMA
    operands = (doc_topics, word_logits, log_norm.reshape(1, width), tile_doc, tile_word, word_counts)
    theta, beta = pl.pallas_call(
        kernel,
        out_shape=(
            jax.ShapeDtypeStruct((n_docs, 128), F32),
            jax.ShapeDtypeStruct((4, n_words, 256), BF16),
        ),
        in_specs=[hbm] * 6,
        out_specs=(vmem, vmem),
        scratch_shapes=[
            V((n_docs, width), BF16),
            V((n_words, width), BF16),
            V((1, width), F32),
            pltpu.SMEM((slots,), jnp.int32),
            pltpu.SMEM((slots,), jnp.int32),
            V(word_counts.shape, jnp.int32),
            V((n_words, width), BF16),
            V((2, 8, WS, DS), BF16),
            V((8, WS, DS), BF16),
            V((8, WS, DS), BF16),
            V((7, WS, DS), BF16),
            V((2, 8, WS, DS), BF16),
            V((n_docs, n_words), BF16),
            V((n_words, n_docs), BF16),
            V((8, n_docs, 128), F32),
            V((14, 2 * DS, 128), BF16),
            V((14, 2 * DS, 128), BF16),
            V((4, n_words, 256), F32),
            V((6, 2 * WS, 256), BF16),
            V((6, 2 * WS, 256), BF16),
            D((7,)),
            D((2,)),
            D((6,)),
            D((1,)),
            D((7,)),
            D((1,)),
            D((14,)),
            D((6,)),
            D((6,)),
        ],
        compiler_params=pltpu.CompilerParams(
            collective_id=0, has_side_effects=True, vmem_limit_bytes=40 << 20
        ),
        name="decoder_gradients",
    )(*(pltpu.with_memory_space_constraint(x, pltpu.HBM) for x in operands))
    return pl.pallas_call(
        finish,
        out_shape=(
            jax.ShapeDtypeStruct((n_docs, 128), F32),
            jax.ShapeDtypeStruct((n_words, width), BF16),
        ),
        in_specs=[pl.BlockSpec(memory_space=pl.ANY)] * 2,
        out_specs=(hbm, hbm),
        scratch_shapes=[D((5,))],
        name="write_out",
    )(*(pltpu.with_memory_space_constraint(x, pltpu.VMEM) for x in (theta, beta)))


def solution(mesh):
    placed = (
        P("doc", "topic"),
        P("vocab", "topic"),
        P("topic"),
        P(("doc", "vocab")),
        P(("doc", "vocab")),
        P(("doc", "vocab"), None, None),
    )
    return jax.shard_map(
        on_device,
        mesh=mesh,
        in_specs=placed,
        out_specs=(P("doc", ("topic", "vocab")), P("vocab", "topic")),
        check_vma=False,
    )
```

time: 290 us -> 44.5 us (0.15)
  waiting for transfers between devices: 212 us -> 0 us
  Pallas kernels: 0 us -> 43.7 us
  other arithmetic: 28.8 us -> 0 us
  matrix products: 19 us -> 0 us
  between operations: 13.9 us -> 0.64 us
  local copies, waits for them, and re-layouts: 12.3 us -> 0 us
    psum x2 -> x0, waiting for transfers between devices: 177 us -> none  [the longest x1 120 us: on_device(): lax.psum(jnp.einsum('gwk,gdk->gwd', word_part, doc_part, preferred_elemen...]
    pallas_call x0 -> x2, Pallas kernels: none -> 43.7 us  [the longest x1 42.8 us: on_device(): pl.pallas_call(kernel, out_shape=(jax.ShapeDtypeStruct((n_docs, 128), F32...]
    unnamed x4 -> x0, waiting for transfers between devices: 35.5 us -> none
    scatter-add x4 -> x0, other arithmetic: 21 us -> none  [the longest x2 11.4 us: accumulate(): theta_acc.at[doc_index].add(toward_theta)]
    dot_general x5 -> x0, matrix products: 19 us -> none  [the longest x2 7.89 us: accumulate(): jnp.einsum('gwd,gwk->gdk', ratio_part, word_part, preferred_element_type=...]
    convert_element_type x5 -> x0, other arithmetic: 6.25 us -> none  [the longest x1 2 us: on_device(): jnp.exp(word_logits.astype(jnp.float32) - log_norm[None, :])]
    unnamed x17 -> x0, local copies, waits for them, and re-layouts: 5.31 us -> none
    gather x2 -> x0, local copies, waits for them, and re-layouts: 4.48 us -> none  [the longest x1 2.76 us: on_device(): doc_rows = topic_blocks[tile_doc]]
  transfers between devices with their start and end apart: 3 -> 0, of which waited for: 3 -> 0; matrix products, arithmetic and copies ran while one was open for 1% -> 0% of each run, Pallas kernels for 0% -> 0%
where the time goes in v3:
time: 44.5 us; the launch traced here: 44.4 us
  Pallas kernels  43.7 us (98%)
  between operations  0.64 us (1%)
    pallas_call x1, Pallas kernels, on_device(): pl.pallas_call(kernel, out_shape=(jax.ShapeDtypeStruct((n_docs, 128), F32...  42.8 us
    pallas_call x1, Pallas kernels, on_device(): pl.pallas_call(finish, out_shape=(jax.ShapeDtypeStruct((n_docs, 128), F32...  0.92 us

profile of v3, /device:TPU:1, one launch (start us, length us, event | category | flops | bytes accessed | tf_op | source)
XLA Modules:
  0.0 44.4 jit_solution(1077743182430584049)
XLA Ops:
  0.6 42.8 %decoder_gradients.1 = (f32[512,128]{1,0:T(8,128)S(1)}, bf16[4,256,256]{2,1,0:T(8,128)(2,1)S(1)}) custom-call(bf16[512,1024]{1,0:T(8,128)(2,1)} %docs_hbm.1, bf16[256,1024]{1,0:T(8,128)(2,1)} %logits_hbm.1, f32[1,1024]{1,0:T(1,128)} %bitcast.1, s32[16]{0:T(128)} %tdoc_hbm.1, s32[16]{0:T(128)} %tword_hbm.1, s32[16,64,128]{2,1,0:T(8,128)} %counts_hbm.1), custom_call_target="tpu_custom_call" | custom-call | tf_op jit(solution)/shard_map/decoder_gradients/pallas_call | solution.py:243
  43.5 0.9 %write_out.1 = (f32[512,128]{1,0:T(8,128)}, bf16[256,1024]{1,0:T(8,128)(2,1)}) custom-call(f32[512,128]{1,0:T(8,128)S(1)} %get-tuple-element.4.th_ref, bf16[4,256,256]{2,1,0:T(8,128)(2,1)S(1)} %get-tuple-element.5.be_ref), custom_call_target="tpu_custom_call" | custom-call | tf_op jit(solution)/shard_map/write_out/pallas_call | solution.py:287

commit v4 on v3

--- a/solution.py
+++ b/solution.py
@@ -23,7 +23,7 @@
     rate_b, c_in, z_out, z_in, rt, rt_t, rw,
     th, y_out, y_in,
     be, x_out, x_in,
-    load_sem, c_sem, send_sem, z_recv, g_recv, f_recv, y_recv, x_recv, a_recv,
+    load_sem, c_sem, send_sem, z_recv, g_recv, f_recv, y_recv, x_recv, a_recv, ready, column,
 ):
     i, t, l = (lax.axis_index(a) for a in ("doc", "topic", "vocab"))
     z, c = lax.div(t, 2), lax.rem(t, 2)
@@ -36,10 +36,11 @@
         pltpu.make_async_copy(tdoc_hbm, tdoc_ref, load_sem.at[5]),
         pltpu.make_async_copy(tword_hbm, tword_ref, load_sem.at[6]),
     ]
-    for cp in loads:
+    for cp in loads[:4]:
         cp.start()
 
     other = (i, 2 * z + 1 - c, l)
+    z_dev = [(i, 2 * k + c, l) for k in range(8)]
     z_at = [lax.rem(z + d, 8) for d in range(8)]
     z_to = [(i, 2 * z_at[d] + c, l) for d in range(8)]
     y_at = [lax.rem(l + d, 8) for d in range(8)]
@@ -47,13 +48,37 @@
     y_to = [(i, t, y_at[1]), (i, t, y_at[7])]
     x_to = [(x_at[1], t, l), (x_at[3], t, l)]
 
+    def signal(sem, dev):
+        pl.semaphore_signal(sem, inc=1, device_id=dev, device_id_type=MESH)
+
     barrier = pltpu.get_barrier_semaphore()
-    partners = z_to[1:] + [other] + y_to + x_to
-    for dev in partners:
-        pl.semaphore_signal(barrier, inc=1, device_id=dev, device_id_type=MESH)
+    signal(barrier, other)
+    for k in range(1, 8):
+        @pl.when(z < k)
+        def _():
+            signal(barrier, z_dev[k])
+
+    @pl.when(z == 0)
+    def _():
+        for dev in y_to + x_to:
+            signal(barrier, dev)
+        pl.semaphore_wait(barrier, 5)
+
+    @pl.when(z > 0)
+    def _():
+        pl.semaphore_wait(barrier, z + 1)
+
+    for k in (3, 2, 4, 1, 5, 0, 6):
+        @pl.when(z > k)
+        def _():
+            signal(ready.at[z], z_dev[k])
 
     def remote(src, dst, send, recv, dev):
         return pltpu.make_async_remote_copy(src, dst, send, recv, device_id=dev, device_id_type=MESH)
+
+    def swap(h):
+        part = pl.ds(4 * h, 4)
+        return remote(rate_b.at[1 - c, part], c_in.at[part], c_sem.at[2], c_sem.at[h], other)
 
     loads[0].wait()
     loads[1].wait()
@@ -67,37 +92,62 @@
             for w in range(WT):
                 p = (2 * h + k) * WT + w
                 rate_b[p % 2, p // 2] = rate[w * WS:(w + 1) * WS, k * DS:(k + 1) * DS]
+        swap(h).start()
+    for cp in loads[4:]:
+        cp.start()
+
+    for h in range(2):
+        part = pl.ds(4 * h, 4)
+        swap(h).wait_recv()
+        z_out[part] = (rate_b[c, part].astype(F32) + c_in[part].astype(F32)).astype(BF16)
+        for k in (3, 2, 1, 0) if h == 0 else (4, 5, 6, 7):
+            @pl.when(z < k)
+            def _():
+                pl.semaphore_wait(ready.at[k], 1)
+
+            @pl.when(z != k)
+            def _():
+                remote(z_out.at[k], z_in.at[z], send_sem.at[0], z_recv.at[0], z_dev[k]).start()
+    z_in[z] = z_out[z]
+
+    @pl.when(z == 0)
+    def _():
+        for dev in y_to + x_to:
+            signal(column.at[0], dev)
+
     for cp in loads[4:]:
         cp.wait()
-
-    pl.semaphore_wait(barrier, len(partners))
-
-    swap = remote(rate_b.at[1 - c], c_in, c_sem.at[0], c_sem.at[1], other)
-    swap.start()
     slot = jnp.int32(0)
     for s in range(tdoc_ref.shape[0]):
         slot = jnp.where(tdoc_ref[s] * WT + tword_ref[s] == t, s, slot)
     count = counts[slot].astype(F32)
-    swap.wait_recv()
-    z_out[...] = (rate_b[c].astype(F32) + c_in[...].astype(F32)).astype(BF16)
-
-    for d in Z_ORDER:
-        remote(z_out.at[z_at[d]], z_in.at[d - 1], send_sem.at[0], z_recv.at[0], z_to[d]).start()
-    total = z_out[z].astype(F32)
-    remote(z_in, z_in, send_sem.at[0], z_recv.at[0], other).wait_recv()
-    for d in range(1, 8):
-        total += z_in[d - 1].astype(F32)
+    seven = z_in.at[pl.ds(0, 7)]
+    remote(seven, seven, send_sem.at[0], z_recv.at[0], other).wait_recv()
+    total = z_in[0].astype(F32)
+    for k in range(1, 8):
+        total += z_in[k].astype(F32)
     rt[c, z] = (-count / (WS * total)).astype(BF16)
 
     mine = rt.at[c, z]
     for d in Z_ORDER:
         remote(mine, mine, send_sem.at[1], g_recv.at[d - 1], z_to[d]).start()
     remote(mine, mine, send_sem.at[2], f_recv.at[0], other).start()
+
+    @pl.when(z == 0)
+    def _():
+        pl.semaphore_wait(column.at[0], 4)
+        for k in range(1, 8):
+            signal(column.at[1], z_dev[k])
+
     for d in Z_ARRIVE:
         tile = rt.at[c, z_at[8 - d]]
         remote(tile, tile, send_sem.at[1], g_recv.at[d - 1], other).wait_recv()
         remote(tile, tile, send_sem.at[2], f_recv.at[0], other).start()
     remote(rt.at[1 - c], rt.at[1 - c], send_sem.at[2], f_recv.at[0], other).wait_recv()
+
+    @pl.when(z > 0)
+    def _():
+        pl.semaphore_wait(column.at[1], 1)
 
     for s in range(DT):
         tiles = [rt[w % 2, 2 * s + w // 2] for w in range(WT)]
@@ -213,9 +263,9 @@
     for way in range(2):
         a_copy(way, 2, x_at[2]).wait_recv()
 
-    remote(rate_b.at[1 - c], c_in, c_sem.at[0], c_sem.at[1], other).wait_send()
-    remote(z_in, z_in, send_sem.at[0], z_recv.at[0], other).wait_send()
-    remote(z_in, z_in, send_sem.at[1], z_recv.at[0], other).wait_send()
+    remote(c_in, c_in, c_sem.at[2], c_sem.at[0], other).wait_send()
+    remote(seven, seven, send_sem.at[0], z_recv.at[0], other).wait_send()
+    remote(seven, seven, send_sem.at[1], z_recv.at[0], other).wait_send()
     remote(z_out, z_out, send_sem.at[2], z_recv.at[0], other).wait_send()
     remote(y_out, y_in, send_sem.at[3], z_recv.at[0], other).wait_send()
     remote(x_out, x_in, send_sem.at[4], z_recv.at[0], other).wait_send()
@@ -259,7 +309,7 @@
             V((2, 8, WS, DS), BF16),
             V((8, WS, DS), BF16),
             V((8, WS, DS), BF16),
-            V((7, WS, DS), BF16),
+            V((8, WS, DS), BF16),
             V((2, 8, WS, DS), BF16),
             V((n_docs, n_words), BF16),
             V((n_words, n_docs), BF16),
@@ -270,7 +320,7 @@
             V((6, 2 * WS, 256), BF16),
             V((6, 2 * WS, 256), BF16),
             D((7,)),
-            D((2,)),
+            D((3,)),
             D((6,)),
             D((1,)),
             D((7,)),
@@ -278,6 +328,8 @@
             D((14,)),
             D((6,)),
             D((6,)),
+            pltpu.SemaphoreType.REGULAR((8,)),
+            pltpu.SemaphoreType.REGULAR((2,)),
         ],
         compiler_params=pltpu.CompilerParams(
             collective_id=0, has_side_effects=True, vmem_limit_bytes=40 << 20

time: 44.5 us -> 43 us (0.966)
  Pallas kernels: 43.7 us -> 42.2 us
    pallas_call x1, Pallas kernels: 42.8 us -> 41.3 us  [on_device(): pl.pallas_call(kernel, out_shape=(jax.ShapeDtypeStruct((n_docs, 128), F32...]
where the time goes in v4:
time: 43 us; the launch traced here: 42.8 us
  Pallas kernels  42.2 us (98%)
  between operations  0.64 us (1%)
    pallas_call x1, Pallas kernels, on_device(): pl.pallas_call(kernel, out_shape=(jax.ShapeDtypeStruct((n_docs, 128), F32...  41.3 us
    pallas_call x1, Pallas kernels, on_device(): pl.pallas_call(finish, out_shape=(jax.ShapeDtypeStruct((n_docs, 128), F32...  0.92 us

profile of v4, /device:TPU:1, one launch (start us, length us, event | category | flops | bytes accessed | tf_op | source)
XLA Modules:
  0.0 42.8 jit_solution(10110906904793398009)
XLA Ops:
  0.6 41.3 %decoder_gradients.1 = (f32[512,128]{1,0:T(8,128)S(1)}, bf16[4,256,256]{2,1,0:T(8,128)(2,1)S(1)}) custom-call(bf16[512,1024]{1,0:T(8,128)(2,1)} %docs_hbm.1, bf16[256,1024]{1,0:T(8,128)(2,1)} %logits_hbm.1, f32[1,1024]{1,0:T(1,128)} %bitcast.1, s32[16]{0:T(128)} %tdoc_hbm.1, s32[16]{0:T(128)} %tword_hbm.1, s32[16,64,128]{2,1,0:T(8,128)} %counts_hbm.1), custom_call_target="tpu_custom_call" | custom-call | tf_op jit(solution)/shard_map/decoder_gradients/pallas_call | solution.py:293
  41.9 0.9 %write_out.1 = (f32[512,128]{1,0:T(8,128)}, bf16[256,1024]{1,0:T(8,128)(2,1)}) custom-call(f32[512,128]{1,0:T(8,128)S(1)} %get-tuple-element.4.th_ref, bf16[4,256,256]{2,1,0:T(8,128)(2,1)S(1)} %get-tuple-element.5.be_ref), custom_call_target="tpu_custom_call" | custom-call | tf_op jit(solution)/shard_map/write_out/pallas_call | solution.py:339

commit v5 on v4

--- a/solution.py
+++ b/solution.py
@@ -229,12 +229,12 @@
     y_go(0, True)
     beta(2)
     x_go(0, True)
+    beta(1)
+    beta(3)
     theta(3)
     theta(5)
+    x_go(1, False)
     y_go(1, False)
-    beta(1)
-    beta(3)
-    x_go(1, False)
     theta(2)
     theta(6)
     beta(0)

time: 43 us -> 43 us (level)
  no operation moved by 1% of the time
where the time goes in v5:
time: 43 us; the launch traced here: 42.8 us
  Pallas kernels  42.2 us (98%)
  between operations  0.64 us (1%)
    pallas_call x1, Pallas kernels, on_device(): pl.pallas_call(kernel, out_shape=(jax.ShapeDtypeStruct((n_docs, 128), F32...  41.3 us
    pallas_call x1, Pallas kernels, on_device(): pl.pallas_call(finish, out_shape=(jax.ShapeDtypeStruct((n_docs, 128), F32...  0.92 us

profile of v5, /device:TPU:1, one launch (start us, length us, event | category | flops | bytes accessed | tf_op | source)
XLA Modules:
  0.0 42.8 jit_solution(15744319485404463064)
XLA Ops:
  0.6 41.3 %decoder_gradients.1 = (f32[512,128]{1,0:T(8,128)S(1)}, bf16[4,256,256]{2,1,0:T(8,128)(2,1)S(1)}) custom-call(bf16[512,1024]{1,0:T(8,128)(2,1)} %docs_hbm.1, bf16[256,1024]{1,0:T(8,128)(2,1)} %logits_hbm.1, f32[1,1024]{1,0:T(1,128)} %bitcast.1, s32[16]{0:T(128)} %tdoc_hbm.1, s32[16]{0:T(128)} %tword_hbm.1, s32[16,64,128]{2,1,0:T(8,128)} %counts_hbm.1), custom_call_target="tpu_custom_call" | custom-call | tf_op jit(solution)/shard_map/decoder_gradients/pallas_call | solution.py:293
  41.9 0.9 %write_out.1 = (f32[512,128]{1,0:T(8,128)}, bf16[256,1024]{1,0:T(8,128)(2,1)}) custom-call(f32[512,128]{1,0:T(8,128)S(1)} %get-tuple-element.4.th_ref, bf16[4,256,256]{2,1,0:T(8,128)(2,1)S(1)} %get-tuple-element.5.be_ref), custom_call_target="tpu_custom_call" | custom-call | tf_op jit(solution)/shard_map/write_out/pallas_call | solution.py:339
